TPU v7x, 128 devices: a whole 4x4x4 slice. The times are simulated.
128 devices in a mesh: dap: 4 (over z_lo, core), dp: 32 (over z_hi, y, x).
Axes of the slice: x: 4, y: 4, z: 4 (z_hi: 2, z_lo: 2; z = z_hi * 2 + z_lo), core: 2. Of those that a mesh axis runs over, the one named last changes fastest.
Arguments:
- pair_rep: bfloat16 [32, 128, 128, 128], P('dp', 'dap'), may hold values from -6 to 6
- cotangent: bfloat16 [32, 128, 128, 128], P('dp', 'dap'), may hold values from -6 to 6
- tok_mask: int32 [32, 128], P('dp'), may hold values from 0 to 1, as said below
- tok_types: int32 [32, 128], P('dp'), may hold values from 0 to 3
- pair_mask: int32 [32, 128, 128], P('dp', 'dap'), may hold values 0 or 1
- triangle_gain: float32 [128], replicated, may hold values from 0.5 to 1.5
- triangle_input: bfloat16 [128, 512], replicated, may hold values from -0.5 to 0.5
- triangle_gating: bfloat16 [128, 128], replicated, may hold values from -0.5 to 0.5
- product_gain: float32 [128], replicated, may hold values from 0.5 to 1.5
- triangle_output: bfloat16 [128, 128], replicated, may hold values from -0.5 to 0.5
- attend_gain: float32 [128], replicated, may hold values from 0.5 to 1.5
- attend_bias: bfloat16 [128, 4], replicated, may hold values from -0.5 to 0.5
- attend_input: bfloat16 [128, 512], replicated, may hold values from -0.5 to 0.5
- attend_output: bfloat16 [128, 128], replicated, may hold values from -0.5 to 0.5
- type_table: float32 [4, 4, 4], replicated, may hold values from -4 to 4
Outputs:
- pair_out: bfloat16 [32, 128, 128, 128], P('dp', 'dap')
- pair_grad: bfloat16 [32, 128, 128, 128], P('dp', 'dap')
- grad_triangle_gain: float32 [128], replicated
- grad_triangle_input: float32 [128, 512], replicated
- grad_triangle_gating: float32 [128, 128], replicated
- grad_product_gain: float32 [128], replicated
- grad_triangle_output: float32 [128, 128], replicated
- grad_attend_gain: float32 [128], replicated
- grad_attend_bias: float32 [128, 4], replicated
- grad_attend_input: float32 [128, 512], replicated
- grad_attend_output: float32 [128, 128], replicated
- grad_type_table: float32 [4, 4, 4], replicated
Inputs may be any that keep to these rules, and one draw needn't show every extreme that they name: `tok_mask`: each crop's real tokens form a leading run of at least 64 tokens.
All inputs are finite; a program needn't handle non-finite values. No bound on the sum of `pair_mask` on one device may be relied on, other than what follows from the above.
Results may differ from a plain program's by a relative error of at most 0.035.
Values may be sent and summed in bfloat16 or wider, within the bound.
A program may use at most 128 MiB of HBM per device.

v0:
```python
from functools import partial
import jax
import jax.numpy as jnp
from jax import lax
from jax.sharding import PartitionSpec as P

EPSILON = 1e-05


def layer_norm(values, scales):
    centred = values - jnp.mean(values, axis=-1, keepdims=True)
    spread = jnp.mean(centred * centred, axis=-1, keepdims=True)
    return centred * lax.rsqrt(spread + EPSILON) * scales


def triangle_first(slab, scales, input_w, gating_w, pair_live):
    channels = slab.shape[-1]
    normed = layer_norm(slab.astype(jnp.float32), scales).astype(jnp.bfloat16)
    projected = jnp.einsum("ijc,cd->ijd", normed, input_w, preferred_element_type=jnp.float32)
    masked = pair_live[..., None]
    left_proj = (
        jax.nn.sigmoid(projected[..., channels : 2 * channels]) * projected[..., :channels] * masked
    ).astype(jnp.bfloat16)
    right_proj = (
        jax.nn.sigmoid(projected[..., 3 * channels :])
        * projected[..., 2 * channels : 3 * channels]
        * masked
    ).astype(jnp.bfloat16)
    out_gate = jax.nn.sigmoid(
        jnp.einsum("ijc,cd->ijd", normed, gating_w, preferred_element_type=jnp.float32)
    )
    return (left_proj, right_proj, out_gate)


def triangle_second(slab, product, out_gate, scales, output_w):
    normed = layer_norm(product, scales).astype(jnp.bfloat16)
    update = out_gate * jnp.einsum(
        "ijc,cd->ijd", normed, output_w, preferred_element_type=jnp.float32
    )
    return (slab.astype(jnp.float32) + update).astype(jnp.bfloat16)


def attend_first(middle, scales, bias_w):
    normed = layer_norm(middle.astype(jnp.float32), scales).astype(jnp.bfloat16)
    bias_rows = jnp.einsum(
        "rjc,ch->hrj", normed, bias_w, preferred_element_type=jnp.float32
    ).astype(jnp.bfloat16)
    return (normed, bias_rows)


def attend_second(middle, normed, bias_all, table, input_w, output_w, one_hot, key_live):
    row_count, length, channels = middle.shape
    head_count = bias_all.shape[0]
    head_size = channels // head_count
    projected = jnp.einsum("ijc,cd->ijd", normed, input_w, preferred_element_type=jnp.float32)
    query = (
        projected[..., :channels]
        .astype(jnp.bfloat16)
        .reshape(row_count, length, head_count, head_size)
    )
    keys_all = (
        projected[..., channels : 2 * channels]
        .astype(jnp.bfloat16)
        .reshape(row_count, length, head_count, head_size)
    )
    values_all = (
        projected[..., 2 * channels : 3 * channels]
        .astype(jnp.bfloat16)
        .reshape(row_count, length, head_count, head_size)
    )
    gate = jax.nn.sigmoid(projected[..., 3 * channels :])
    type_bias = jnp.einsum("ja,hab,kb->hjk", one_hot, table, one_hot)
    scores = jnp.einsum(
        "rjhd,rkhd->rhjk", query, keys_all, preferred_element_type=jnp.float32
    ) / jnp.sqrt(jnp.float32(head_size))
    scores = scores + (bias_all + type_bias)[None]
    exponent = jnp.exp(scores) * key_live[:, None, None, :]
    totals = jnp.maximum(jnp.sum(exponent, axis=-1, keepdims=True), 1.0)
    weights = (exponent / totals).astype(jnp.bfloat16)
    attended = jnp.einsum(
        "rhjk,rkhd->rjhd", weights, values_all, preferred_element_type=jnp.float32
    ).reshape(row_count, length, channels)
    gated = (gate * attended).astype(jnp.bfloat16)
    update = jnp.einsum("ijc,cd->ijd", gated, output_w, preferred_element_type=jnp.float32)
    return (middle.astype(jnp.float32) + update).astype(jnp.bfloat16)


def per_device(
    pair_rep,
    cotangent,
    tok_mask,
    tok_types,
    pair_mask,
    triangle_gain,
    triangle_input,
    triangle_gating,
    product_gain,
    triangle_output,
    attend_gain,
    attend_bias,
    attend_input,
    attend_output,
    type_table,
):
    slab = pair_rep[0]
    row_count = slab.shape[0]
    length = slab.shape[1]
    tokens = tok_mask[0].astype(jnp.float32)
    first_row = lax.axis_index("dap") * row_count
    row_tokens = lax.dynamic_slice_in_dim(tokens, first_row, row_count)
    pair_live = pair_mask[0].astype(jnp.float32) * row_tokens[:, None] * tokens[None, :]
    one_hot = (
        tok_types[0][:, None] == jnp.arange(type_table.shape[1], dtype=jnp.int32)[None, :]
    ).astype(jnp.float32)
    first_out, first_back = jax.vjp(
        partial(triangle_first, pair_live=pair_live),
        slab,
        triangle_gain,
        triangle_input,
        triangle_gating,
    )
    left_proj, right_proj, out_gate = first_out
    right_all = lax.all_gather(right_proj, "dap", axis=0, tiled=True)
    product = jnp.einsum("ikc,jkc->ijc", left_proj, right_all, preferred_element_type=jnp.float32)
    middle, second_back = jax.vjp(
        triangle_second, slab, product, out_gate, product_gain, triangle_output
    )
    third_out, third_back = jax.vjp(attend_first, middle, attend_gain, attend_bias)
    normed, bias_rows = third_out
    bias_all = lax.all_gather(bias_rows, "dap", axis=1, tiled=True).astype(jnp.float32)
    pair_out, fourth_back = jax.vjp(
        partial(attend_second, one_hot=one_hot, key_live=pair_live),
        middle,
        normed,
        bias_all,
        type_table,
        attend_input,
        attend_output,
    )
    d_middle_a, d_normed, d_bias_all, d_table, d_att_in, d_att_out = fourth_back(cotangent[0])
    d_bias_rows = lax.psum_scatter(
        d_bias_all.astype(jnp.bfloat16), "dap", scatter_dimension=1, tiled=True
    )
    d_middle_b, d_att_gain, d_att_bias = third_back((d_normed, d_bias_rows))
    attend_terms = (
        d_att_gain,
        d_att_bias.astype(jnp.float32),
        d_att_in.astype(jnp.float32),
        d_att_out.astype(jnp.float32),
        d_table,
    )
    d_middle = d_middle_a + d_middle_b
    d_slab_c, d_product, d_gate, d_prod_gain, d_tri_out = second_back(d_middle)
    d_left = jnp.einsum(
        "ijc,jkc->ikc", d_product, right_all, preferred_element_type=jnp.float32
    ).astype(jnp.bfloat16)
    d_right = lax.psum_scatter(
        jnp.einsum("ijc,ikc->jkc", d_product, left_proj, preferred_element_type=jnp.float32).astype(
            jnp.bfloat16
        ),
        "dap",
        scatter_dimension=0,
        tiled=True,
    ).astype(jnp.float32)
    d_right = d_right.astype(jnp.bfloat16)
    d_slab_d, d_tri_gain, d_tri_in, d_tri_gate = first_back((d_left, d_right, d_gate))
    d_slab = d_slab_c + d_slab_d
    triangle_terms = (
        d_tri_gain,
        d_tri_in.astype(jnp.float32),
        d_tri_gate.astype(jnp.float32),
        d_prod_gain,
        d_tri_out.astype(jnp.float32),
    )
    summed_all = lax.psum(triangle_terms + attend_terms, ("dap", "dp"))
    triangle_summed = summed_all[:5]
    attend_summed = summed_all[5:]
    factor = (length * length * lax.axis_size("dp")) ** (-0.5)
    return (
        pair_out[None],
        d_slab[None],
        triangle_summed[0] * factor,
        triangle_summed[1] * factor,
        triangle_summed[2] * factor,
        triangle_summed[3] * factor,
        triangle_summed[4] * factor,
        attend_summed[0] * factor,
        attend_summed[1] * factor,
        attend_summed[2] * factor,
        attend_summed[3] * factor,
        attend_summed[4] * factor,
    )


def solution(mesh):
    return jax.shard_map(
        per_device,
        mesh=mesh,
        in_specs=(
            P("dp", "dap", None, None),
            P("dp", "dap", None, None),
            P("dp", None),
            P("dp", None),
            P("dp", "dap", None),
            P(),
            P(),
            P(),
            P(),
            P(),
            P(),
            P(),
            P(),
            P(),
            P(),
        ),
        out_specs=(
            P("dp", "dap", None, None),
            P("dp", "dap", None, None),
            P(),
            P(),
            P(),
            P(),
            P(),
            P(),
            P(),
            P(),
            P(),
            P(),
        ),
        check_vma=False,
    )
```

profile of v0, /device:TPU:1, one launch (start us, length us, event | category | flops | bytes accessed | tf_op | source)
XLA Modules:
  0.0 484.0 jit_solution(14713057218166650713)
XLA Ops:
  7.3 1.7 copy.124
  11.1 2.7 multiply_convert_fusion.1
  18.8 47.5 %all-gather.2.cloned.1.call-done = bf16[128,128,128]{2,1,0:T(8,128)(2,1)} async-done(((bf16[32,128,128]{2,1,0:T(8,128)(2,1)}), bf16[128,128,128]{2,1,0:T(8,128)(2,1)}) %all-gather.2.cloned.1.call-update) | async-done | bytes 4194320 | tf_op jit(solution)/shard_map/all_gather | solution.py:123
  66.3 6.7 %copy.133 = bf16[128,128,128]{1,0,2:T(8,128)(2,1)} copy(bf16[128,128,128]{2,1,0:T(8,128)(2,1)} %all-gather.2.cloned.1.call-done) | data formatting | bytes 8388608 | tf_op jit(solution)/shard_map/all_gather | solution.py:123
  73.1 4.8 bitcast_reduce_fusion
  79.7 2.5 convert_reduce_fusion
  82.6 3.3 fusion.166
  86.0 1.6 slice.39
  87.6 2.9 copy.206
  90.5 3.7 fusion.164
  94.2 2.3 copy.139
  96.5 1.7 fusion.93
  98.1 5.6 %all_gather.7 = bf16[4,128,128]{2,0,1:T(4,128)(2,1)S(1)} all-gather(bf16[4,32,128]{2,0,1:T(4,128)(2,1)S(1)} %fusion.93), channel_id=1, replica_groups=mesh['dap'=4,'dp'=32] {'dap'}, dimensions={1}, use_global_device_ids=true | all-gather | bytes 163840 | tf_op jit(solution)/shard_map/all_gather | solution.py:130
  105.8 2.4 copy.140
  108.2 2.3 copy.141
  110.4 4.3 multiply_reduce_fusion
  114.8 1.6 convert_multiply_fusion.9
  116.4 4.5 fusion.4
  121.0 5.5 %fusion.161 = (bf16[4,128,128]{1,2,0:T(8,128)(2,1)S(1)}, f32[32,4,128,128]{2,3,1,0:T(8,128)S(1)}, bf16[32,4,128,128]{2,3,1,0:T(8,128)(2,1)S(1)}) fusion(f32[4,128,128]{1,2,0:T(8,128)} %copy-done.27, f32[32,4,128,128]{2,3,1,0:T(8,128)S(1)} %get-tuple-element.96, f32[32,128]{1,0:T(8,128)S(1)} %copy-done.44, f32[32,4,128]{2,1,0:T(4,128)S(1)} %get-tuple-element.84, ...), kind=kLoop, calls=%fused_computation.231 | loop fusion | flops 23003136 | bytes 25706496 | tf_op jit(solution)/shard_map/transpose(jvp())/reduce_sum | solution.py:76
  126.5 3.5 fusion.70
  130.0 3.3 fusion.67
  133.4 2.5 fusion.167
  135.9 3.3 fusion.168
  140.2 4.6 fusion.41
  144.8 1.4 copy-done.25
  146.3 1.7 fusion.65
  148.0 28.9 %all-reduce.14.cloned.1.call-done = bf16[4,128,128]{2,0,1:T(4,128)(2,1)} async-done(((bf16[4,128,128]{2,0,1:T(4,128)(2,1)}), bf16[4,128,128]{2,0,1:T(4,128)(2,1)}) %all-reduce.14.cloned.1.call-update) | async-done | bytes 131088
  176.9 2.5 fusion.47
  179.5 2.0 fusion.42
  183.9 1.9 fusion.44
  188.2 3.3 fusion.63
  191.5 6.8 %copy.160 = bf16[128,128,128]{1,0,2:T(8,128)(2,1)} copy(bf16[128,128,128]{2,1,0:T(8,128)(2,1)} %fusion.63) | data formatting | bytes 8388608 | tf_op jit(solution)/shard_map/ijc,ikc->jkc/dot_general | solution.py:158
  199.9 1.5 fusion.77
  201.3 2.3 copy.172
  203.8 2.4 fusion.90
  206.3 3.9 fusion.85
  210.2 1.4 fusion.95
  213.4 1.5 fusion.88
  217.5 27.1 %reduce-scatter.2.cloned.1.call-done = bf16[32,128,128]{1,2,0:T(8,128)(2,1)} async-done(((bf16[128,128,128]{1,2,0:T(8,128)(2,1)}), bf16[32,128,128]{1,2,0:T(8,128)(2,1)}) %reduce-scatter.2.cloned.1.call-update) | async-done | bytes 1048592 | tf_op jit(solution)/shard_map/reduce_scatter | solution.py:157
  244.7 5.1 %fusion.60 = (f32[32,128,128]{1,2,0:T(8,128)S(1)}, f32[32,128,128]{1,2,0:T(8,128)S(1)}, f32[32,128,128]{1,2,0:T(8,128)S(1)}, f32[32,128,128]{1,2,0:T(8,128)S(1)}) fusion(bf16[32,128,128]{1,2,0:T(8,128)(2,1)} %reduce-scatter.2.cloned.1.call-done, f32[32,128]{1,0:T(8,128)S(1)} %copy-done.45, f32[32,128,512]{1,2,0:T(8,128)} %copy-done.2, ...), kind=kLoop, calls=%fused_computation.101 | loop fusion | flops 10485760 | bytes 18890752 | tf_op jit(solution)/shard_map/transpose(jvp())/mul | solution.py:25
  250.7 2.2 fusion.83
  253.0 3.3 fusion.39
  256.3 1.5 fusion.45
  260.2 65.8 %all-reduce.9 = (f32[128]{0:T(128)S(1)}, f32[128]{0:T(128)S(1)}, f32[128]{0:T(128)S(1)}, f32[128,4]{0,1:T(4,128)S(1)}, f32[4,4,4]{1,2,0:T(4,128)S(1)}) all-reduce(f32[128]{0:T(128)S(1)} %get-tuple-element.52, f32[128]{0:T(128)S(1)} %get-tuple-element.48, f32[128]{0:T(128)S(1)} %copy-done.70, ...), channel_id=1, replica_groups=mesh['dap'=4,'dp'=32] {'dap','dp'}, use_global_device_ids=true, to_apply=%region_18.0 | all-reduce | flops 960 | bytes 7680 | tf_op jit(solution)/shard_map/psum | solution.py:175
  328.4 144.0 %all-reduce.16.cloned.1.call-done = (f32[128,512]{1,0:T(8,128)}, f32[128,128]{1,0:T(8,128)}, f32[128,128]{1,0:T(8,128)}, f32[128,512]{1,0:T(8,128)}, f32[128,128]{1,0:T(8,128)}) async-done(((f32[128,512]{1,0:T(8,128)}, f32[128,128]{1,0:T(8,128)}, f32[128,128]{1,0:T(8,128)}, f32[128,512]{1,0:T(8,128)}, f32[128,128]{1,0:T(8,128)}), (f32[128,512]{1,0:T(8,128)}, f32[128,128]{1,0:T(8,128)}, ...) | async-done | bytes 720912 | tf_op jit(solution)/shard_map/psum | solution.py:175
  472.4 1.5 broadcast_multiply_fusion.4
  473.9 1.9 broadcast_multiply_fusion
  475.7 1.5 broadcast_multiply_fusion.2
  (203 shorter events, 28.4 us)
Async XLA Ops:
  7.2 75.4 %copy-start = (bf16[128,512]{1,0:T(8,128)(2,1)S(1)}, bf16[128,512]{1,0:T(8,128)(2,1)}, u32[]{:S(2)}) copy-start(bf16[128,512]{1,0:T(8,128)(2,1)} %param.27) | copy-start | bytes 393220
  7.2 59.1 %all-gather.2.cloned.1.call-start = ((), (), s32[]{:S(2)}) async-start(), calls=%async_computation.1 | async-start | bytes 5242880 | tf_op jit(solution)/shard_map/all_gather | solution.py:123
  7.2 2.3 copy-start.73
  7.3 2.4 copy-start.52
  7.3 2.4 copy-start.61
  9.6 69.8 %copy-start.33 = (f32[32,128]{1,0:T(8,128)}, f32[32,128]{1,0:T(8,128)S(1)}, u32[]{:S(2)}) copy-start(f32[32,128]{1,0:T(8,128)S(1)} %fusion.126) | copy-start | bytes 49156
  11.0 3.6 copy-start.2
  11.1 3.5 copy-start.43
  15.9 2.8 copy-start.63
  16.0 160.9 %all-reduce.14.cloned.1.call-start = ((), (), s32[]{:S(2)}) async-start(), calls=%async_computation.3 | async-start | bytes 262144
  78.9 3.3 copy-start.16
  79.7 2.5 copy-start.13
  79.7 3.0 copy-start.68
  82.2 3.8 copy-start.8
  82.2 14.2 %copy-start.35 = (f32[32,128]{1,0:T(8,128)}, f32[32,128]{1,0:T(8,128)S(1)}, u32[]{:S(2)}) copy-start(f32[32,128]{1,0:T(8,128)S(1)} %broadcast_multiply_fusion.5) | copy-start | bytes 49156
  82.6 3.4 copy-start.50
  82.6 13.8 %copy-start.39 = (f32[32,128]{1,0:T(8,128)}, f32[32,128]{1,0:T(8,128)S(1)}, u32[]{:S(2)}) copy-start(f32[32,128]{1,0:T(8,128)S(1)} %fusion.128) | copy-start | bytes 49156
  94.2 2.3 copy-start.71
  105.8 10.6 %copy-start.27 = (f32[4,128,128]{1,2,0:T(8,128)}, f32[4,128,128]{1,2,0:T(8,128)S(1)}, u32[]{:S(2)}) copy-start(f32[4,128,128]{1,2,0:T(8,128)S(1)} %copy.145) | copy-start | bytes 786436
  110.4 4.3 copy-start.19
  110.4 4.3 copy-start.24
  110.4 4.3 copy-start.56
  116.4 4.6 copy-start.31
  126.5 3.5 copy-start.22
  133.4 2.5 copy-start.32
  140.0 104.7 %reduce-scatter.2.cloned.1.call-start = ((), (), s32[]{:S(2)}) async-start(), calls=%async_computation.2 | async-start | bytes 5242880 | tf_op jit(solution)/shard_map/reduce_scatter | solution.py:157
  140.2 6.0 %copy-start.28 = (bf16[32,4,128,32]{2,3,1,0:T(8,128)(2,1)S(1)}, bf16[32,4,128,32]{2,3,1,0:T(8,128)(2,1)}, u32[]{:S(2)}) copy-start(bf16[32,4,128,32]{2,3,1,0:T(8,128)(2,1)} %fusion.70) | copy-start | bytes 3145732
  140.2 6.0 %copy-start.29 = (bf16[32,4,128,32]{2,3,1,0:T(8,128)(2,1)S(1)}, bf16[32,4,128,32]{2,3,1,0:T(8,128)(2,1)}, u32[]{:S(2)}) copy-start(bf16[32,4,128,32]{2,3,1,0:T(8,128)(2,1)} %fusion.67) | copy-start | bytes 3145732
  140.2 6.0 %copy-start.30 = (bf16[32,4,32,128]{3,2,1,0:T(8,128)(2,1)S(1)}, bf16[32,4,32,128]{3,2,1,0:T(8,128)(2,1)}, u32[]{:S(2)}) copy-start(bf16[32,4,32,128]{3,2,1,0:T(8,128)(2,1)} %fusion.168) | copy-start | bytes 3145732
  146.2 30.7 %copy-start.36 = (f32[32,128]{1,0:T(8,128)S(1)}, f32[32,128]{1,0:T(8,128)}, u32[]{:S(2)}) copy-start(f32[32,128]{1,0:T(8,128)} %copy-done.35) | copy-start | bytes 49156
  146.2 30.7 %copy-start.69 = (f32[128]{0:T(128)S(1)}, f32[128]{0:T(128)}, u32[]{:S(2)}) copy-start(f32[128]{0:T(128)} %param.25) | copy-start | bytes 1540
  146.2 30.7 %copy-start.72 = (bf16[128,4]{0,1:T(4,128)(2,1)S(1)}, bf16[128,4]{0,1:T(4,128)(2,1)}, u32[]{:S(2)}) copy-start(bf16[128,4]{0,1:T(4,128)(2,1)} %param.26) | copy-start | bytes 3076
  148.0 31.4 %copy-start.51 = (f32[32,128]{1,0:T(8,128)S(1)}, f32[32,128]{1,0:T(8,128)}, u32[]{:S(2)}) copy-start(f32[32,128]{1,0:T(8,128)} %copy-done.50) | copy-start | bytes 49156
  148.0 31.5 %copy-start.40 = (f32[32,128]{1,0:T(8,128)S(1)}, f32[32,128]{1,0:T(8,128)}, u32[]{:S(2)}) copy-start(f32[32,128]{1,0:T(8,128)} %copy-done.39) | copy-start | bytes 49156
  176.9 2.6 copy-start.9
  176.9 4.6 copy-start.20
  185.8 2.4 copy-start.15
  198.3 274.0 %all-reduce.16.cloned.1.call-start = ((), (), s32[]{:S(2)}) async-start(), calls=%async_computation.4 | async-start | bytes 1441792 | tf_op jit(solution)/shard_map/psum | solution.py:175
  199.9 3.7 copy-start.64
  203.8 2.4 copy-start.26
  206.3 5.3 %copy-start.7 = (f32[32,128,128]{1,2,0:T(8,128)S(1)}, f32[32,128,128]{1,2,0:T(8,128)}, u32[]{:S(2)}) copy-start(f32[32,128,128]{1,2,0:T(8,128)} %get-tuple-element.90) | copy-start | bytes 6291460
  213.3 2.3 copy-start.3
  213.3 3.0 copy-start.12
  216.3 28.3 %copy-start.45 = (f32[32,128]{1,0:T(8,128)S(1)}, f32[32,128]{1,0:T(8,128)}, u32[]{:S(2)}) copy-start(f32[32,128]{1,0:T(8,128)} %copy-done.43) | copy-start | bytes 49156
  217.5 32.2 %copy-start.53 = (bf16[128,512]{1,0:T(8,128)(2,1)S(1)}, bf16[128,512]{1,0:T(8,128)(2,1)}, u32[]{:S(2)}) copy-start(bf16[128,512]{1,0:T(8,128)(2,1)} %param.21) | copy-start | bytes 393220
  250.7 2.3 copy-start.59
  253.0 3.3 copy-start.47
  257.8 219.4 %copy-start.1 = (bf16[128,512]{1,0:T(8,128)(2,1)S(1)}, bf16[128,512]{1,0:T(8,128)(2,1)}, u32[]{:S(2)}) copy-start(bf16[128,512]{1,0:T(8,128)(2,1)} %param.27) | copy-start | bytes 393220
  (31 other events, 40.3 us)
Sparse Core Ops, SparseCore 0:
  16.1 50.2 all-gather.1
  140.1 36.7 all-reduce.13
  198.5 46.1 reduce-scatter.1
  327.4 144.9 all-reduce.15
where the time goes:
time: 494 us; the launch traced here: 484 us
  waiting for transfers between devices  248 us (50%)
  blocking collectives  71.4 us (14%)
  matrix products  66.2 us (13%)
  local copies, waits for them, and re-layouts  48.2 us (10%)
  other arithmetic  34.7 us (7%)
  between operations  15.4 us (3%)
    psum x1, waiting for transfers between devices, per_device(): summed_all = lax.psum(triangle_terms + attend_terms, ('dap', 'dp'))  144 us
    psum x1, blocking collectives, per_device(): summed_all = lax.psum(triangle_terms + attend_terms, ('dap', 'dp'))  65.8 us
    all_gather x1, waiting for transfers between devices, per_device(): right_all = lax.all_gather(right_proj, 'dap', axis=0, tiled=True)  47.5 us
    unnamed x5, waiting for transfers between devices  29 us
    reduce_scatter x1, waiting for transfers between devices, per_device(): lax.psum_scatter(jnp.einsum('ijc,ikc->jkc', d_product, left_proj, preferr...  27.1 us
    unnamed x158, local copies, waits for them, and re-layouts  19.2 us
    dot_general x3, matrix products, attend_second(): jnp.einsum('rjhd,rkhd->rhjk', query, keys_all, preferred_element_type=jnp...  11.1 us
    dot_general x3, matrix products, attend_second(): jnp.einsum('rhjk,rkhd->rjhd', weights, values_all, preferred_element_type...  10.3 us
  transfers between devices with their start and end apart: 4, of which 4 were waited for; matrix products, arithmetic and copies ran while one was open for 5% of the time, Pallas kernels for 0%

commit v1 on v0

--- a/solution.py
+++ b/solution.py
@@ -172,7 +172,7 @@
         d_prod_gain,
         d_tri_out.astype(jnp.float32),
     )
-    summed_all = lax.psum(triangle_terms + attend_terms, ("dap", "dp"))
+    summed_all = lax.psum(lax.psum(triangle_terms + attend_terms, "dp"), "dap")
     triangle_summed = summed_all[:5]
     attend_summed = summed_all[5:]
     factor = (length * length * lax.axis_size("dp")) ** (-0.5)

time: 494 us -> 670 us (1.36)
  blocking collectives: 71.4 us -> 197 us
  waiting for transfers between devices: 248 us -> 295 us
    psum x1 -> x2, blocking collectives: 65.8 us -> 192 us  [per_device(): summed_all = lax.psum(lax.psum(triangle_terms + attend_terms, 'dp'), 'dap')]
    psum x1 -> x2, waiting for transfers between devices: 144 us -> 192 us  [per_device(): summed_all = lax.psum(lax.psum(triangle_terms + attend_terms, 'dp'), 'dap')]
    unnamed x158 -> x156, local copies, waits for them, and re-layouts: 19.2 us -> 20.2 us
    unnamed x5 -> x6, waiting for transfers between devices: 29 us -> 29 us
  transfers between devices with their start and end apart: 4 -> 5, of which waited for: 4 -> 5; matrix products, arithmetic and copies ran while one was open for 5% -> 5% of each run, Pallas kernels for 0% -> 0%
where the time goes in v1:
time: 670 us; the launch traced here: 660 us
  waiting for transfers between devices  295 us (44%)
  blocking collectives  197 us (29%)
  matrix products  67.2 us (10%)
  local copies, waits for them, and re-layouts  49.1 us (7%)
  other arithmetic  35.2 us (5%)
  between operations  15.4 us (2%)
    psum x2, blocking collectives, per_device(): summed_all = lax.psum(lax.psum(triangle_terms + attend_terms, 'dp'), 'dap')  192 us
    psum x2, waiting for transfers between devices, per_device(): summed_all = lax.psum(lax.psum(triangle_terms + attend_terms, 'dp'), 'dap')  192 us
    all_gather x1, waiting for transfers between devices, per_device(): right_all = lax.all_gather(right_proj, 'dap', axis=0, tiled=True)  47.5 us
    unnamed x6, waiting for transfers between devices  29 us
    reduce_scatter x1, waiting for transfers between devices, per_device(): lax.psum_scatter(jnp.einsum('ijc,ikc->jkc', d_product, left_proj, preferr...  27.2 us
    unnamed x156, local copies, waits for them, and re-layouts  20.2 us
  transfers between devices with their start and end apart: 5, of which 5 were waited for; matrix products, arithmetic and copies ran while one was open for 5% of the time, Pallas kernels for 0%

profile of v1, /device:TPU:1, one launch (start us, length us, event | category | flops | bytes accessed | tf_op | source)
XLA Modules:
  0.0 660.1 jit_solution(11335494049353224839)
XLA Ops:
  7.3 1.7 copy.124
  11.1 2.7 multiply_convert_fusion.1
  18.8 47.5 %all-gather.2.cloned.1.call-done = bf16[128,128,128]{2,1,0:T(8,128)(2,1)} async-done(((bf16[32,128,128]{2,1,0:T(8,128)(2,1)}), bf16[128,128,128]{2,1,0:T(8,128)(2,1)}) %all-gather.2.cloned.1.call-update) | async-done | bytes 4194320 | tf_op jit(solution)/shard_map/all_gather | solution.py:123
  66.4 6.7 %copy.133 = bf16[128,128,128]{1,0,2:T(8,128)(2,1)} copy(bf16[128,128,128]{2,1,0:T(8,128)(2,1)} %all-gather.2.cloned.1.call-done) | data formatting | bytes 8388608 | tf_op jit(solution)/shard_map/all_gather | solution.py:123
  73.1 4.8 bitcast_reduce_fusion
  79.7 2.5 convert_reduce_fusion
  82.7 3.3 fusion.166
  86.0 1.6 slice.39
  87.7 2.9 copy.206
  90.6 3.7 fusion.164
  94.2 2.3 copy.139
  96.5 1.7 fusion.93
  98.2 5.6 all_gather.7
  105.8 2.4 copy.140
  108.2 2.3 copy.141
  110.5 4.3 multiply_reduce_fusion
  114.9 1.6 convert_multiply_fusion.9
  116.5 4.5 fusion.4
  121.1 5.5 fusion.161
  126.6 3.5 fusion.70
  130.1 3.3 fusion.67
  133.4 2.5 fusion.167
  136.0 3.3 fusion.168
  140.3 4.6 fusion.41
  146.3 1.7 fusion.65
  148.0 28.9 %all-reduce.17.cloned.1.call-done = bf16[4,128,128]{2,0,1:T(4,128)(2,1)} async-done(((bf16[4,128,128]{2,0,1:T(4,128)(2,1)}), bf16[4,128,128]{2,0,1:T(4,128)(2,1)}) %all-reduce.17.cloned.1.call-update) | async-done | bytes 131088
  177.0 2.5 fusion.47
  179.5 1.5 fusion.42
  183.4 1.9 fusion.44
  187.8 3.3 fusion.63
  191.1 6.7 %copy.160 = bf16[128,128,128]{1,0,2:T(8,128)(2,1)} copy(bf16[128,128,128]{2,1,0:T(8,128)(2,1)} %fusion.63) | data formatting | bytes 8388608 | tf_op jit(solution)/shard_map/ijc,ikc->jkc/dot_general | solution.py:158
  200.8 2.3 copy.172
  203.3 2.4 fusion.90
  205.8 3.9 fusion.85
  212.9 1.5 fusion.88
  217.0 27.2 %reduce-scatter.2.cloned.1.call-done = bf16[32,128,128]{1,2,0:T(8,128)(2,1)} async-done(((bf16[128,128,128]{1,2,0:T(8,128)(2,1)}), bf16[32,128,128]{1,2,0:T(8,128)(2,1)}) %reduce-scatter.2.cloned.1.call-update) | async-done | bytes 1048592 | tf_op jit(solution)/shard_map/reduce_scatter | solution.py:157
  244.2 5.1 fusion.60
  249.3 1.7 fusion.66
  251.0 2.2 fusion.83
  253.3 3.5 fusion.39
  258.4 157.6 %all-reduce.9 = (f32[128]{0:T(128)S(1)}, f32[128]{0:T(128)S(1)}, f32[128]{0:T(128)S(1)}, f32[128,4]{0,1:T(4,128)S(1)}, f32[4,4,4]{1,2,0:T(4,128)S(1)}) all-reduce(f32[128]{0:T(128)S(1)} %get-tuple-element.52, f32[128]{0:T(128)S(1)} %get-tuple-element.48, f32[128]{0:T(128)S(1)} %get-tuple-element.50, ...), channel_id=1, replica_groups=mesh['dap'=4,'dp'=32] {'dp'}, use_global_device_ids=true, to_apply=%region_18.0 | all-reduce | flops 960 | bytes 7680 | tf_op jit(solution)/shard_map/psum | solution.py:175
  416.0 34.2 %all-reduce.11 = (f32[128]{0:T(128)S(1)}, f32[128]{0:T(128)S(1)}, f32[128]{0:T(128)S(1)}, f32[128,4]{0,1:T(4,128)S(1)}, f32[4,4,4]{1,2,0:T(4,128)S(1)}) all-reduce(f32[128]{0:T(128)S(1)} %get-tuple-element.54, f32[128]{0:T(128)S(1)} %get-tuple-element.55, f32[128]{0:T(128)S(1)} %get-tuple-element.56, ...), channel_id=1, replica_groups=mesh['dap'=4,'dp'=32] {'dap'}, use_global_device_ids=true, to_apply=%region_19.0 | all-reduce | flops 960 | bytes 7680 | tf_op jit(solution)/shard_map/psum | solution.py:175
  450.1 2.0 fusion.98
  452.2 132.2 %all-reduce.19.cloned.1.call-done = (f32[128,512]{1,0:T(8,128)}, f32[128,128]{1,0:T(8,128)}, f32[128,128]{1,0:T(8,128)}, f32[128,512]{1,0:T(8,128)}, f32[128,128]{1,0:T(8,128)}) async-done(((f32[128,512]{1,0:T(8,128)}, f32[128,128]{1,0:T(8,128)}, f32[128,128]{1,0:T(8,128)}, f32[128,512]{1,0:T(8,128)}, f32[128,128]{1,0:T(8,128)}), (f32[128,512]{1,0:T(8,128)}, f32[128,128]{1,0:T(8,128)}, ...) | async-done | bytes 720912 | tf_op jit(solution)/shard_map/psum | solution.py:175
  584.5 2.3 copy.173
  589.1 59.4 %all-reduce.21.cloned.1.call-done = (f32[128,512]{1,0:T(8,128)}, f32[128,128]{1,0:T(8,128)}, f32[128,128]{1,0:T(8,128)}, f32[128,512]{1,0:T(8,128)}, f32[128,128]{1,0:T(8,128)}) async-done(((f32[128,512]{1,0:T(8,128)}, f32[128,128]{1,0:T(8,128)}, f32[128,128]{1,0:T(8,128)}, f32[128,512]{1,0:T(8,128)}, f32[128,128]{1,0:T(8,128)}), (f32[128,512]{1,0:T(8,128)}, f32[128,128]{1,0:T(8,128)}, ...) | async-done | bytes 720912 | tf_op jit(solution)/shard_map/psum | solution.py:175
  649.9 1.9 broadcast_multiply_fusion
  651.8 1.5 broadcast_multiply_fusion.2
  (205 shorter events, 32.3 us)
Async XLA Ops:
  7.2 75.5 %copy-start = (bf16[128,512]{1,0:T(8,128)(2,1)S(1)}, bf16[128,512]{1,0:T(8,128)(2,1)}, u32[]{:S(2)}) copy-start(bf16[128,512]{1,0:T(8,128)(2,1)} %param.27) | copy-start | bytes 393220
  7.2 59.2 %all-gather.2.cloned.1.call-start = ((), (), s32[]{:S(2)}) async-start(), calls=%async_computation.1 | async-start | bytes 5242880 | tf_op jit(solution)/shard_map/all_gather | solution.py:123
  7.2 2.3 copy-start.72
  7.3 2.4 copy-start.52
  7.3 2.4 copy-start.61
  9.6 69.9 %copy-start.33 = (f32[32,128]{1,0:T(8,128)}, f32[32,128]{1,0:T(8,128)S(1)}, u32[]{:S(2)}) copy-start(f32[32,128]{1,0:T(8,128)S(1)} %fusion.126) | copy-start | bytes 49156
  11.0 3.6 copy-start.2
  11.1 3.5 copy-start.43
  15.9 2.8 copy-start.63
  16.0 161.0 %all-reduce.17.cloned.1.call-start = ((), (), s32[]{:S(2)}) async-start(), calls=%async_computation.3 | async-start | bytes 262144
  78.9 3.3 copy-start.16
  79.7 2.5 copy-start.13
  79.7 3.0 copy-start.68
  82.3 3.8 copy-start.8
  82.3 14.2 %copy-start.35 = (f32[32,128]{1,0:T(8,128)}, f32[32,128]{1,0:T(8,128)S(1)}, u32[]{:S(2)}) copy-start(f32[32,128]{1,0:T(8,128)S(1)} %broadcast_multiply_fusion.5) | copy-start | bytes 49156
  82.6 3.4 copy-start.50
  82.7 13.8 %copy-start.39 = (f32[32,128]{1,0:T(8,128)}, f32[32,128]{1,0:T(8,128)S(1)}, u32[]{:S(2)}) copy-start(f32[32,128]{1,0:T(8,128)S(1)} %fusion.128) | copy-start | bytes 49156
  94.2 2.3 copy-start.70
  105.8 10.7 %copy-start.27 = (f32[4,128,128]{1,2,0:T(8,128)}, f32[4,128,128]{1,2,0:T(8,128)S(1)}, u32[]{:S(2)}) copy-start(f32[4,128,128]{1,2,0:T(8,128)S(1)} %copy.145) | copy-start | bytes 786436
  110.5 4.3 copy-start.19
  110.5 4.3 copy-start.24
  110.5 4.3 copy-start.56
  116.5 4.5 copy-start.31
  126.6 3.5 copy-start.22
  133.4 2.5 copy-start.32
  140.0 104.1 %reduce-scatter.2.cloned.1.call-start = ((), (), s32[]{:S(2)}) async-start(), calls=%async_computation.2 | async-start | bytes 5242880 | tf_op jit(solution)/shard_map/reduce_scatter | solution.py:157
  140.3 6.0 copy-start.28
  140.3 6.0 copy-start.29
  140.3 6.0 copy-start.30
  146.3 30.7 %copy-start.36 = (f32[32,128]{1,0:T(8,128)S(1)}, f32[32,128]{1,0:T(8,128)}, u32[]{:S(2)}) copy-start(f32[32,128]{1,0:T(8,128)} %copy-done.35) | copy-start | bytes 49156
  146.3 30.7 %copy-start.69 = (f32[128]{0:T(128)S(1)}, f32[128]{0:T(128)}, u32[]{:S(2)}) copy-start(f32[128]{0:T(128)} %param.25) | copy-start | bytes 1540
  146.3 30.7 %copy-start.71 = (bf16[128,4]{0,1:T(4,128)(2,1)S(1)}, bf16[128,4]{0,1:T(4,128)(2,1)}, u32[]{:S(2)}) copy-start(bf16[128,4]{0,1:T(4,128)(2,1)} %param.26) | copy-start | bytes 3076
  148.0 31.5 %copy-start.51 = (f32[32,128]{1,0:T(8,128)S(1)}, f32[32,128]{1,0:T(8,128)}, u32[]{:S(2)}) copy-start(f32[32,128]{1,0:T(8,128)} %copy-done.50) | copy-start | bytes 49156
  148.0 31.5 %copy-start.40 = (f32[32,128]{1,0:T(8,128)S(1)}, f32[32,128]{1,0:T(8,128)}, u32[]{:S(2)}) copy-start(f32[32,128]{1,0:T(8,128)} %copy-done.39) | copy-start | bytes 49156
  177.0 2.6 copy-start.9
  177.0 4.1 copy-start.20
  185.4 2.4 copy-start.15
  197.8 386.6 %all-reduce.19.cloned.1.call-start = ((), (), s32[]{:S(2)}) async-start(), calls=%async_computation.4 | async-start | bytes 1441792 | tf_op jit(solution)/shard_map/psum | solution.py:175
  199.4 3.7 copy-start.64
  203.3 2.4 copy-start.26
  205.8 5.3 copy-start.7
  212.9 2.3 copy-start.3
  212.9 3.0 copy-start.12
  215.8 28.4 %copy-start.45 = (f32[32,128]{1,0:T(8,128)S(1)}, f32[32,128]{1,0:T(8,128)}, u32[]{:S(2)}) copy-start(f32[32,128]{1,0:T(8,128)} %copy-done.43) | copy-start | bytes 49156
  217.0 32.3 %copy-start.53 = (bf16[128,512]{1,0:T(8,128)(2,1)S(1)}, bf16[128,512]{1,0:T(8,128)(2,1)}, u32[]{:S(2)}) copy-start(bf16[128,512]{1,0:T(8,128)(2,1)} %param.21) | copy-start | bytes 393220
  253.3 3.6 copy-start.47
  256.9 391.6 %all-reduce.21.cloned.1.call-start = ((), (), s32[]{:S(2)}) async-start(), calls=%async_computation.5 | async-start | bytes 1441792 | tf_op jit(solution)/shard_map/psum | solution.py:175
  584.4 68.9 %copy-start.1 = (bf16[128,512]{1,0:T(8,128)(2,1)S(1)}, bf16[128,512]{1,0:T(8,128)(2,1)}, u32[]{:S(2)}) copy-start(bf16[128,512]{1,0:T(8,128)(2,1)} %param.27) | copy-start | bytes 393220
  (31 other events, 41.2 us)
Sparse Core Ops, SparseCore 0:
  16.1 50.2 all-gather.1
  140.2 36.7 all-reduce.16
  198.0 46.1 reduce-scatter.1
  257.0 327.3 all-reduce.18
  587.4 61.0 all-reduce.20
